TPU v7x, 32 devices: a whole 2x2x4 slice. The times are simulated.
32 devices in a mesh: blk: 8 (over z, x), mblk: 4 (over y, core).
Axes of the slice: x: 2, y: 2, z: 4, core: 2. Of those that a mesh axis runs over, the one named last changes fastest.
Arguments:
- alm: bfloat16 [3, 2, 2048, 8192], P(None, None, 'mblk', 'blk'), may hold values from -6 to 6
- legendre: bfloat16 [2048, 40, 8192], P('mblk', None, 'blk'), may hold values from -0.0625 to 0.0625
- m_value: int32 [2048], replicated, may hold values from 0 to 2047, each once
- cycle_weight: float32 [40], P('blk'), may hold values from 0.5 to 2
Outputs:
- bispec_alm: bfloat16 [2, 2048, 8192], P(None, 'mblk', 'blk')
Inputs may be any that keep to these rules, and one draw needn't show every extreme that they name: m_value holds each order from 0 to 2047 exactly once.
All inputs are finite; a program needn't handle non-finite values.
Results may differ from a plain program's by a relative error of at most 0.0049.
Values may be sent and summed in bfloat16 or wider, within the bound.
No kernel may reach another device: no remote copies, remote signals or barrier semaphores. Data moves between devices by JAX's collectives and lax.ppermute only.
A program may use at most 128 MiB of HBM per device.

v0:
```python
import math

import jax
import jax.numpy as jnp
from jax import lax
from jax.sharding import PartitionSpec as P

M = 2048
NPHI = 32768


def wave_table(orders, pixels):
    products = orders[:, None] * pixels[None, :] % NPHI
    angles = products.astype(jnp.float32) * (2.0 * math.pi / NPHI)
    return (jnp.cos(angles), jnp.sin(angles))


def split_parts(spectra):
    order_count = spectra.shape[2]
    values = spectra.reshape(spectra.shape[0], 3, 2, order_count)
    return (values[:, :, 0], values[:, :, 1])


def cycle_maps(real_part, imag_part, orders, pixel_first, pixel_count):
    row_total = real_part.shape[0]
    order_count = orders.shape[0]
    left_side = jnp.concatenate([real_part, imag_part], axis=2).reshape(
        row_total * 3, 2 * order_count
    )
    pix_block = math.gcd(pixel_count, max(1, 2**20 // order_count))

    def one_block(offset):
        pixels = offset + lax.iota(jnp.int32, pix_block)
        cosine, sine_rows = wave_table(orders, pixels)
        wave_rows = jnp.concatenate([cosine, -sine_rows], axis=0)
        return jnp.dot(
            left_side,
            wave_rows,
            precision=lax.Precision.HIGHEST,
            preferred_element_type=jnp.float32,
        )

    offsets = pixel_first + pix_block * jnp.arange(pixel_count // pix_block, dtype=jnp.int32)
    blocks = lax.map(one_block, offsets)
    return jnp.moveaxis(blocks, 0, 1).reshape(row_total, 3, pixel_count)


def pixel_sums(product, orders):
    row_total = product.shape[0]
    order_count = orders.shape[0]
    pixel_count = product.shape[1]
    pix_block = math.gcd(pixel_count, max(1, 2**20 // order_count))

    def add_block(number, running):
        part_rows = lax.dynamic_slice_in_dim(product, number * pix_block, pix_block, 1)
        pixels = number * pix_block + lax.iota(jnp.int32, pix_block)
        cosine, sine_rows = wave_table(orders, pixels)
        wave_rows = jnp.concatenate([cosine, -sine_rows], axis=0)
        return running + lax.dot_general(
            part_rows,
            wave_rows,
            (((1,), (1,)), ((), ())),
            precision=lax.Precision.HIGHEST,
            preferred_element_type=jnp.float32,
        )

    running = lax.fori_loop(
        0, pixel_count // pix_block, add_block, jnp.zeros((row_total, 2 * order_count), jnp.float32)
    )
    return running.reshape(row_total, 2, order_count)


def shards(alm, legendre, m_value, cycle_weight):
    m_dev = legendre.shape[0]
    cycle_count = legendre.shape[1]
    l_dev = legendre.shape[2]
    pixel_dev = NPHI // lax.axis_size("mblk")
    coeffs = alm.reshape(6, m_dev, l_dev)
    own_first = lax.axis_index("mblk") * m_dev
    own_orders = lax.dynamic_slice_in_dim(m_value, own_first, m_dev)
    pixel_first = lax.axis_index("mblk") * pixel_dev
    leg_table = legendre
    partial_value = lax.dot_general(
        coeffs, leg_table, (((2,), (2,)), ((1,), (0,))), preferred_element_type=jnp.float32
    )
    spectra = lax.psum_scatter(
        jnp.transpose(partial_value, (2, 1, 0)), "blk", scatter_dimension=0, tiled=True
    )
    real_part, imag_part = split_parts(lax.all_gather(spectra, "mblk", axis=2, tiled=True))
    cycle_map = cycle_maps(real_part, imag_part, m_value, pixel_first, pixel_dev)
    cycle_map = cycle_map * (1.0 / math.sqrt(M))
    product = cycle_map[:, 0] * cycle_map[:, 1] * cycle_map[:, 2]
    order_sums = pixel_sums(lax.all_gather(product, "mblk", axis=1, tiled=True), own_orders)
    scale_rows = cycle_weight[:, None] * (1.0 / math.sqrt(NPHI))
    real_sum = order_sums[:, 0]
    imag_sum = order_sums[:, 1]
    weighted = jnp.stack([real_sum * scale_rows, imag_sum * scale_rows], axis=1).astype(
        jnp.bfloat16
    )
    leg_table = legendre
    result = lax.dot_general(
        lax.all_gather(weighted, "blk", axis=0, tiled=True),
        leg_table,
        (((0,), (1,)), ((2,), (0,))),
        preferred_element_type=jnp.float32,
    )
    scale_factor = math.sqrt(l_dev * lax.axis_size("blk") / cycle_count)
    return (jnp.transpose(result, (1, 0, 2)) * scale_factor).astype(jnp.bfloat16)


def solution(mesh):
    in_specs = (P(None, None, "mblk", "blk"), P("mblk", None, "blk"), P(), P("blk"))
    out_specs = P(None, "mblk", "blk")
    return jax.shard_map(shards, mesh=mesh, in_specs=in_specs, out_specs=out_specs, check_vma=False)
```

profile of v0, /device:TPU:0, one launch (start us, length us, event | category | flops | bytes accessed | tf_op | source)
XLA Modules:
  0.0 975.3 jit_solution(4530559573645057220)
XLA Ops:
  6.5 18.2 %fusion.32 = f32[40,6,512]{0,1,2:T(8,128)S(1)} fusion(bf16[512,40,1024]{2,1,0:T(8,128)(2,1)} %param.9, bf16[6,512,1024]{2,1,0:T(8,128)(2,1)} %bitcast.27), kind=kOutput, calls=%fused_computation.41 | convolution fusion | flops 251658240 | bytes 48726016 | tf_op jit(solution)/shard_map/dot_general | solution.py:83
  26.7 65.5 %reduce-scatter.2.cloned.1.call-done = f32[5,6,512]{2,1,0:T(8,128)} async-done(((f32[40,6,512]{2,1,0:T(8,128)}), f32[5,6,512]{2,1,0:T(8,128)}) %reduce-scatter.2.cloned.1.call-update) | async-done | bytes 61456 | tf_op jit(solution)/shard_map/reduce_scatter | solution.py:86
  99.4 358.3 %while.28 = (s32[]{:T(128)}, f32[16,15,512]{2,1,0:T(8,128)S(1)}, s32[2048]{0:T(1024)S(1)}, s32[16]{0:T(128)S(1)}, f32[15,4096]{1,0:T(8,128)S(1)}, /*index=5*/s32[]{:T(128)}) while((s32[]{:T(128)}, f32[16,15,512]{2,1,0:T(8,128)S(1)}, s32[2048]{0:T(1024)S(1)}, s32[16]{0:T(128)S(1)}, f32[15,4096]{1,0:T(8,128)S(1)}, /*index=5*/s32[]{:T(128)}) %tuple.78), condition=%wide.region_2.3_spmd, body=%wide.region_1.2_spmd.sunk | while | flops 395313664 | bytes 17084504 | solution.py:44
  100.8 16.6 %fusion.51 = (f32[2048,512]{1,0:T(8,128)S(1)}, f32[2048,512]{1,0:T(8,128)S(1)}) fusion(s32[512]{0:T(512)S(1)} %iota_add_fusion.4, s32[2048]{0:T(1024)S(1)} %get-tuple-element.303), kind=kLoop, calls=%fused_computation.13.clone.1 | loop fusion | flops 15728640 | bytes 8398848 | tf_op jit(solution)/shard_map/while/body/eval_jaxpr/cos | solution.py:15
  145.6 16.6 %fusion.51 = (f32[2048,512]{1,0:T(8,128)S(1)}, f32[2048,512]{1,0:T(8,128)S(1)}) fusion(s32[512]{0:T(512)S(1)} %iota_add_fusion.4, s32[2048]{0:T(1024)S(1)} %get-tuple-element.303), kind=kLoop, calls=%fused_computation.13.clone.1 | loop fusion | flops 15728640 | bytes 8398848 | tf_op jit(solution)/shard_map/while/body/eval_jaxpr/cos | solution.py:15
  467.1 451.4 %while.29 = (s32[]{:T(128)}, f32[5,1024]{1,0:T(8,128)S(1)}, f32[5,32768]{1,0:T(8,128)S(1)}, s32[512]{0:T(512)S(1)}, s32[]{:T(128)}, /*index=5*/s32[]{:T(128)}, s32[]{:T(128)}, s32[]{:T(128)}) while((s32[]{:T(128)}, f32[5,1024]{1,0:T(8,128)S(1)}, f32[5,32768]{1,0:T(8,128)S(1)}, s32[512]{0:T(512)S(1)}, s32[]{:T(128)}, ...), condition=%wide.region_4.5_spmd.clone, body=%wide.region_3.4_spmd.clone.sunk | while | flops 143667200 | bytes 16914580 | solution.py:67
  467.1 18.9 %fusion.55 = (f32[512,2048]{1,0:T(8,128)}, f32[512,2048]{1,0:T(8,128)}) fusion(s32[2048]{0:T(1024)S(1)} %iota_add_fusion.5, s32[512]{0:T(512)S(1)} %get-tuple-element.326), kind=kLoop, calls=%fused_computation.31.clone.1 | loop fusion | flops 15728640 | bytes 8398848 | tf_op jit(solution)/shard_map/while/body/eval_jaxpr/cos | solution.py:15
  495.3 18.9 %fusion.55 = (f32[512,2048]{1,0:T(8,128)}, f32[512,2048]{1,0:T(8,128)}) fusion(s32[2048]{0:T(1024)S(1)} %iota_add_fusion.5, s32[512]{0:T(512)S(1)} %get-tuple-element.326), kind=kLoop, calls=%fused_computation.31.clone.1 | loop fusion | flops 15728640 | bytes 8398848 | tf_op jit(solution)/shard_map/while/body/eval_jaxpr/cos | solution.py:15
  523.5 18.9 %fusion.55 = (f32[512,2048]{1,0:T(8,128)}, f32[512,2048]{1,0:T(8,128)}) fusion(s32[2048]{0:T(1024)S(1)} %iota_add_fusion.5, s32[512]{0:T(512)S(1)} %get-tuple-element.326), kind=kLoop, calls=%fused_computation.31.clone.1 | loop fusion | flops 15728640 | bytes 8398848 | tf_op jit(solution)/shard_map/while/body/eval_jaxpr/cos | solution.py:15
  551.7 18.9 %fusion.55 = (f32[512,2048]{1,0:T(8,128)}, f32[512,2048]{1,0:T(8,128)}) fusion(s32[2048]{0:T(1024)S(1)} %iota_add_fusion.5, s32[512]{0:T(512)S(1)} %get-tuple-element.326), kind=kLoop, calls=%fused_computation.31.clone.1 | loop fusion | flops 15728640 | bytes 8398848 | tf_op jit(solution)/shard_map/while/body/eval_jaxpr/cos | solution.py:15
  580.0 18.9 %fusion.55 = (f32[512,2048]{1,0:T(8,128)}, f32[512,2048]{1,0:T(8,128)}) fusion(s32[2048]{0:T(1024)S(1)} %iota_add_fusion.5, s32[512]{0:T(512)S(1)} %get-tuple-element.326), kind=kLoop, calls=%fused_computation.31.clone.1 | loop fusion | flops 15728640 | bytes 8398848 | tf_op jit(solution)/shard_map/while/body/eval_jaxpr/cos | solution.py:15
  608.2 18.9 %fusion.55 = (f32[512,2048]{1,0:T(8,128)}, f32[512,2048]{1,0:T(8,128)}) fusion(s32[2048]{0:T(1024)S(1)} %iota_add_fusion.5, s32[512]{0:T(512)S(1)} %get-tuple-element.326), kind=kLoop, calls=%fused_computation.31.clone.1 | loop fusion | flops 15728640 | bytes 8398848 | tf_op jit(solution)/shard_map/while/body/eval_jaxpr/cos | solution.py:15
  636.4 18.9 %fusion.55 = (f32[512,2048]{1,0:T(8,128)}, f32[512,2048]{1,0:T(8,128)}) fusion(s32[2048]{0:T(1024)S(1)} %iota_add_fusion.5, s32[512]{0:T(512)S(1)} %get-tuple-element.326), kind=kLoop, calls=%fused_computation.31.clone.1 | loop fusion | flops 15728640 | bytes 8398848 | tf_op jit(solution)/shard_map/while/body/eval_jaxpr/cos | solution.py:15
  664.6 18.9 %fusion.55 = (f32[512,2048]{1,0:T(8,128)}, f32[512,2048]{1,0:T(8,128)}) fusion(s32[2048]{0:T(1024)S(1)} %iota_add_fusion.5, s32[512]{0:T(512)S(1)} %get-tuple-element.326), kind=kLoop, calls=%fused_computation.31.clone.1 | loop fusion | flops 15728640 | bytes 8398848 | tf_op jit(solution)/shard_map/while/body/eval_jaxpr/cos | solution.py:15
  692.8 18.9 %fusion.55 = (f32[512,2048]{1,0:T(8,128)}, f32[512,2048]{1,0:T(8,128)}) fusion(s32[2048]{0:T(1024)S(1)} %iota_add_fusion.5, s32[512]{0:T(512)S(1)} %get-tuple-element.326), kind=kLoop, calls=%fused_computation.31.clone.1 | loop fusion | flops 15728640 | bytes 8398848 | tf_op jit(solution)/shard_map/while/body/eval_jaxpr/cos | solution.py:15
  721.0 18.9 %fusion.55 = (f32[512,2048]{1,0:T(8,128)}, f32[512,2048]{1,0:T(8,128)}) fusion(s32[2048]{0:T(1024)S(1)} %iota_add_fusion.5, s32[512]{0:T(512)S(1)} %get-tuple-element.326), kind=kLoop, calls=%fused_computation.31.clone.1 | loop fusion | flops 15728640 | bytes 8398848 | tf_op jit(solution)/shard_map/while/body/eval_jaxpr/cos | solution.py:15
  749.2 18.9 %fusion.55 = (f32[512,2048]{1,0:T(8,128)}, f32[512,2048]{1,0:T(8,128)}) fusion(s32[2048]{0:T(1024)S(1)} %iota_add_fusion.5, s32[512]{0:T(512)S(1)} %get-tuple-element.326), kind=kLoop, calls=%fused_computation.31.clone.1 | loop fusion | flops 15728640 | bytes 8398848 | tf_op jit(solution)/shard_map/while/body/eval_jaxpr/cos | solution.py:15
  777.4 18.9 %fusion.55 = (f32[512,2048]{1,0:T(8,128)}, f32[512,2048]{1,0:T(8,128)}) fusion(s32[2048]{0:T(1024)S(1)} %iota_add_fusion.5, s32[512]{0:T(512)S(1)} %get-tuple-element.326), kind=kLoop, calls=%fused_computation.31.clone.1 | loop fusion | flops 15728640 | bytes 8398848 | tf_op jit(solution)/shard_map/while/body/eval_jaxpr/cos | solution.py:15
  805.6 18.9 %fusion.55 = (f32[512,2048]{1,0:T(8,128)}, f32[512,2048]{1,0:T(8,128)}) fusion(s32[2048]{0:T(1024)S(1)} %iota_add_fusion.5, s32[512]{0:T(512)S(1)} %get-tuple-element.326), kind=kLoop, calls=%fused_computation.31.clone.1 | loop fusion | flops 15728640 | bytes 8398848 | tf_op jit(solution)/shard_map/while/body/eval_jaxpr/cos | solution.py:15
  833.8 18.9 %fusion.55 = (f32[512,2048]{1,0:T(8,128)}, f32[512,2048]{1,0:T(8,128)}) fusion(s32[2048]{0:T(1024)S(1)} %iota_add_fusion.5, s32[512]{0:T(512)S(1)} %get-tuple-element.326), kind=kLoop, calls=%fused_computation.31.clone.1 | loop fusion | flops 15728640 | bytes 8398848 | tf_op jit(solution)/shard_map/while/body/eval_jaxpr/cos | solution.py:15
  862.0 18.9 %fusion.55 = (f32[512,2048]{1,0:T(8,128)}, f32[512,2048]{1,0:T(8,128)}) fusion(s32[2048]{0:T(1024)S(1)} %iota_add_fusion.5, s32[512]{0:T(512)S(1)} %get-tuple-element.326), kind=kLoop, calls=%fused_computation.31.clone.1 | loop fusion | flops 15728640 | bytes 8398848 | tf_op jit(solution)/shard_map/while/body/eval_jaxpr/cos | solution.py:15
  890.3 18.9 %fusion.55 = (f32[512,2048]{1,0:T(8,128)}, f32[512,2048]{1,0:T(8,128)}) fusion(s32[2048]{0:T(1024)S(1)} %iota_add_fusion.5, s32[512]{0:T(512)S(1)} %get-tuple-element.326), kind=kLoop, calls=%fused_computation.31.clone.1 | loop fusion | flops 15728640 | bytes 8398848 | tf_op jit(solution)/shard_map/while/body/eval_jaxpr/cos | solution.py:15
  918.6 30.5 %all_gather.11 = bf16[40,2,512]{2,1,0:T(2,128)(2,1)S(1)} all-gather(bf16[5,2,512]{2,1,0:T(2,128)(2,1)S(1)} %pad_maximum_fusion.1), channel_id=1, replica_groups=mesh['blk'=8,'mblk'=4] {'blk'}, dimensions={0}, use_global_device_ids=true | all-gather | bytes 92160 | tf_op jit(solution)/shard_map/all_gather | solution.py:102
  949.3 17.2 %fusion.31 = bf16[2,512,1024]{2,0,1:T(2,128)(2,1)S(1)} fusion(bf16[40,2,512]{0,1,2:T(2,128)(2,1)S(1)} %copy.18, bf16[512,40,1024]{2,1,0:T(8,128)(2,1)} %param.9), kind=kOutput, calls=%fused_computation.40 | convolution fusion | flops 85983232 | bytes 44122112 | tf_op jit(solution)/shard_map/dot_general | solution.py:101
  (123 shorter events, 493.1 us)
Async XLA Ops:
  6.5 85.6 %reduce-scatter.2.cloned.1.call-start = ((), (), s32[]{:S(2)}) async-start(), calls=%async_computation.1 | async-start | bytes 737280 | tf_op jit(solution)/shard_map/reduce_scatter | solution.py:86
  6.5 20.0 %copy-start = (s32[2048]{0:T(1024)S(1)}, s32[2048]{0:T(1024)}, u32[]{:S(2)}) copy-start(s32[2048]{0:T(1024)} %param.10) | copy-start | bytes 24580
  6.5 20.1 %copy-start.1 = (f32[5]{0:T(128)S(1)}, f32[5]{0:T(128)}, u32[]{:S(2)}) copy-start(f32[5]{0:T(128)} %param.11) | copy-start | bytes 64
Sparse Core Ops, SparseCore 0:
  26.6 65.4 reduce-scatter.1
where the time goes:
time: 976 us; the launch traced here: 975 us
  other arithmetic  580 us (59%)
  matrix products  255 us (26%)
  waiting for transfers between devices  65.5 us (7%)
  blocking collectives  44.8 us (5%)
  local copies, waits for them, and re-layouts  15.4 us (2%)
  between operations  13.5 us (1%)
    cos x32, other arithmetic, wave_table(): return (jnp.cos(angles), jnp.sin(angles))  569 us
    dot_general x16, matrix products, add_block(): lax.dot_general(part_rows, wave_rows, (((1,), (1,)), ((), ())), precision...  148 us
    dot_general x16, matrix products, one_block(): jnp.dot(left_side, wave_rows, precision=lax.Precision.HIGHEST, preferred_...  72 us
    reduce_scatter x1, waiting for transfers between devices, shards(): lax.psum_scatter(jnp.transpose(partial_value, (2, 1, 0)), 'blk', scatter_...  65.5 us
    all_gather x1, blocking collectives, shards(): lax.all_gather(weighted, 'blk', axis=0, tiled=True)  30.5 us
  transfers between devices with their start and end apart: 1, of which 1 were waited for; matrix products, arithmetic and copies ran while one was open for 0% of the time, Pallas kernels for 0%

commit v1 on v0

v1 whole, which is shorter than its diff:
```python
import math

import jax
import jax.numpy as jnp
import numpy as np
from jax import lax
from jax.experimental import pallas as pl
from jax.experimental.pallas import tpu as pltpu
from jax.sharding import PartitionSpec as P

NPHI = 32768
LANES = 128

f32 = jnp.float32
bf16 = jnp.bfloat16


def grid_size(order_count):
    size = LANES
    while size <= 4 * (order_count - 1):
        size *= 2
    return min(size, NPHI)


def split_np(table):
    high = table.astype(jnp.bfloat16)
    low = (table - high.astype(np.float64)).astype(jnp.bfloat16)
    return high, low


def fourier_tables(order_count):
    size = grid_size(order_count)
    n2 = LANES
    n1 = size // n2
    k1 = order_count // n2
    turn = 2.0 * np.pi
    ang1 = turn * (np.outer(np.arange(n1), np.arange(k1)) % n1) / n1
    c1, s1 = np.cos(ang1), np.sin(ang1)
    ang2 = turn * (np.outer(np.arange(n2), np.arange(n2)) % n2) / n2
    c2, s2 = np.cos(ang2), np.sin(ang2)
    angt = turn * np.outer(np.arange(n1), np.arange(n2)) / size
    first = np.block([[c1, -s1], [s1, c1]])
    second = np.concatenate([c2, -s2], axis=0)
    third = np.concatenate([c2, -s2], axis=1)
    fourth = np.block([[c1.T, s1.T], [-s1.T, c1.T]])
    h, l = split_np(first)
    first3 = np.concatenate([h, h, l], axis=1)
    h, l = split_np(second)
    second3 = np.concatenate([h, h, l], axis=0)
    h, l = split_np(third)
    third3 = np.concatenate([h, h, l], axis=0)
    h, l = split_np(fourth)
    fourth3 = np.concatenate([h, h, l], axis=1)
    twiddle = np.stack([np.cos(angt), np.sin(angt)]).astype(np.float32)
    return first3, second3, third3, fourth3, twiddle


def split2(value):
    high = value.astype(bf16)
    low = (value - high.astype(f32)).astype(bf16)
    return high, low


def mm(a, b):
    return jnp.dot(a, b, preferred_element_type=f32)


def band_kernel(
    spec_ref, order_ref, own_ref, weight_ref, first_ref, second_ref, third_ref, fourth_ref, twid_ref,
    out_ref, high_ref, low_ref, *, cycles, order_count, copies,
):
    blocks, rows, width = spec_ref.shape
    n2 = LANES
    k1 = order_count // n2
    n1 = twid_ref.shape[1]
    orders = order_ref[...]
    mask1 = lax.broadcasted_iota(jnp.int32, (k1, order_count), 0) == orders // n2
    hot2 = (lax.broadcasted_iota(jnp.int32, (n2, order_count), 0) == orders % n2).astype(f32).astype(bf16)
    for row in range(rows):
        for block in range(blocks):
            lanes = slice(block * width, (block + 1) * width)
            value = spec_ref[block, row : row + 1, :]
            high = value.astype(bf16).astype(f32)
            low = value - high
            chosen = mask1[:, lanes]
            high_ref[row * k1 : (row + 1) * k1, lanes] = jnp.where(chosen, high, 0.0).astype(bf16)
            low_ref[row * k1 : (row + 1) * k1, lanes] = jnp.where(chosen, low, 0.0).astype(bf16)
    contract = (((1,), (1,)), ((), ()))
    ordered = lax.dot_general(high_ref[...], hot2, contract, preferred_element_type=f32)
    ordered = ordered + lax.dot_general(low_ref[...], hot2, contract, preferred_element_type=f32)
    first = first_ref[...]
    second = second_ref[...]
    third = third_ref[...]
    fourth = fourth_ref[...]
    cosine = twid_ref[0]
    sine = twid_ref[1]
    scale = 1.0 / math.sqrt(order_count)
    results = []
    for cycle in range(cycles):
        maps = None
        for field in range(3):
            start = (cycle * 3 + field) * 2 * k1
            high, low = split2(ordered[start : start + 2 * k1, :])
            part = mm(first, jnp.concatenate([high, low, high], axis=0))
            re, im = part[:n1], part[n1:]
            turned = jnp.concatenate([re * cosine - im * sine, re * sine + im * cosine], axis=1)
            high, low = split2(turned)
            cycle_map = mm(jnp.concatenate([high, low, high], axis=1), second) * scale
            maps = cycle_map if maps is None else maps * cycle_map
        high, low = split2(maps)
        part = mm(jnp.concatenate([high, low, high], axis=1), third)
        re, im = part[:, :n2], part[:, n2:]
        turned = jnp.concatenate([re * cosine + im * sine, im * cosine - re * sine], axis=0)
        high, low = split2(turned)
        sums = mm(fourth, jnp.concatenate([high, low, high], axis=0))
        results.append(sums * weight_ref[0, cycle])
    sums = jnp.concatenate(results, axis=0)
    high, low = split2(sums)
    own = own_ref[...]
    own_width = own.shape[1]
    own1 = lax.broadcasted_iota(jnp.int32, (k1, own_width), 0) == own // n2
    own2 = (lax.broadcasted_iota(jnp.int32, (n2, own_width), 0) == own % n2).astype(f32).astype(bf16)
    picked = mm(high, own2) + mm(low, own2)
    parts = []
    for row in range(2 * cycles):
        chosen = jnp.where(own1, picked[row * k1 : (row + 1) * k1, :], 0.0)
        parts.append(jnp.sum(chosen, axis=0, keepdims=True))
    weighted = jnp.concatenate(parts, axis=0).astype(bf16)
    for copy in range(copies):
        out_ref[copy] = weighted


def band_step(spectra, orders, own_orders, weights, cycles, copies):
    order_count = orders.shape[0]
    tables = fourier_tables(order_count)
    rows = spectra.shape[1]
    own = own_orders.shape[0]
    k1 = order_count // LANES
    vmem = pl.BlockSpec(memory_space=pltpu.VMEM)
    return pl.pallas_call(
        lambda *refs: band_kernel(*refs, cycles=cycles, order_count=order_count, copies=copies),
        out_shape=jax.ShapeDtypeStruct((copies, 2 * cycles, own), bf16),
        in_specs=[vmem, vmem, vmem, pl.BlockSpec(memory_space=pltpu.SMEM)] + [vmem] * 5,
        out_specs=vmem,
        scratch_shapes=[pltpu.VMEM((rows * k1, order_count), bf16)] * 2,
        compiler_params=pltpu.CompilerParams(vmem_limit_bytes=24 * 2**20),
        name="band",
    )(spectra, orders[None, :], own_orders[None, :], weights[None, :], *tables)


def shards(alm, legendre, m_value, cycle_weight):
    m_dev, cycle_count, l_dev = legendre.shape
    bands = lax.axis_size("blk")
    cycles = cycle_count // bands
    order_count = m_value.shape[0]
    coeffs = alm.reshape(6, m_dev, l_dev)
    own_orders = lax.dynamic_slice_in_dim(m_value, lax.axis_index("mblk") * m_dev, m_dev)
    partial_value = lax.dot_general(
        coeffs, legendre, (((2,), (2,)), ((1,), (0,))), preferred_element_type=f32
    )
    outgoing = jnp.transpose(partial_value, (2, 1, 0)).reshape(bands, cycles * 6, m_dev).astype(bf16)
    incoming = lax.all_to_all(outgoing, "blk", 0, 0, tiled=True)
    spectra = jnp.sum(incoming.astype(f32), axis=0)
    gathered = lax.all_gather(spectra, "mblk", axis=0)
    weights = cycle_weight * (NPHI / grid_size(order_count) / math.sqrt(NPHI))
    copies = band_step(gathered, m_value, own_orders, weights, cycles, bands)
    weighted = lax.all_to_all(copies, "blk", 0, 0, tiled=True)
    result = lax.dot_general(
        weighted.reshape(cycle_count, 2, m_dev),
        legendre,
        (((0,), (1,)), ((2,), (0,))),
        preferred_element_type=f32,
    )
    scale_factor = math.sqrt(l_dev * bands / cycle_count)
    return (jnp.transpose(result, (1, 0, 2)) * scale_factor).astype(bf16)


def solution(mesh):
    in_specs = (P(None, None, "mblk", "blk"), P("mblk", None, "blk"), P(), P("blk"))
    out_specs = P(None, "mblk", "blk")
    return jax.shard_map(shards, mesh=mesh, in_specs=in_specs, out_specs=out_specs, check_vma=False)
```

time: 976 us -> 80 us (0.08)
  other arithmetic: 580 us -> 0.05 us
  matrix products: 255 us -> 35.7 us
  waiting for transfers between devices: 65.5 us -> 8.83 us
  blocking collectives: 44.8 us -> 16.7 us
  between operations: 13.5 us -> 0.09 us
  local copies, waits for them, and re-layouts: 15.4 us -> 4.09 us
    cos x32 -> x0, other arithmetic: 569 us -> none  [wave_table(): return (jnp.cos(angles), jnp.sin(angles))]
    dot_general x34 -> x2, matrix products: 255 us -> 35.7 us  [the longest x1 18.6 us: shards(): lax.dot_general(coeffs, legendre, (((2,), (2,)), ((1,), (0,))), preferred...]
    reduce_scatter x1 -> x0, waiting for transfers between devices: 65.5 us -> none  [shards(): lax.psum_scatter(jnp.transpose(partial_value, (2, 1, 0)), 'blk', scatter_...]
    all_gather x3 -> x1, blocking collectives: 44.8 us -> 5.78 us  [shards(): gathered = lax.all_gather(spectra, 'mblk', axis=0)]
    all_to_all x0 -> x1, blocking collectives: none -> 10.9 us  [shards(): weighted = lax.all_to_all(copies, 'blk', 0, 0, tiled=True)]
    add x33 -> x0, other arithmetic: 10.4 us -> none  [the longest x16 10.3 us: one_block(): pixels = offset + lax.iota(jnp.int32, pix_block)]
where the time goes in v1:
time: 80 us; the launch traced here: 79.7 us
  matrix products  35.7 us (45%)
  blocking collectives  16.7 us (21%)
  waiting for transfers between devices  8.83 us (11%)
  starting transfers between devices  7.3 us (9%)
  Pallas kernels  6.97 us (9%)
  local copies, waits for them, and re-layouts  4.09 us (5%)
    dot_general x1, matrix products, shards(): lax.dot_general(coeffs, legendre, (((2,), (2,)), ((1,), (0,))), preferred...  18.6 us
    dot_general x1, matrix products, shards(): lax.dot_general(weighted.reshape(cycle_count, 2, m_dev), legendre, (((0,)...  17.2 us
    all_to_all x1, blocking collectives, shards(): weighted = lax.all_to_all(copies, 'blk', 0, 0, tiled=True)  10.9 us
    all_to_all x1, waiting for transfers between devices, shards(): incoming = lax.all_to_all(outgoing, 'blk', 0, 0, tiled=True)  8.83 us
    all_to_all x1, starting transfers between devices, shards(): incoming = lax.all_to_all(outgoing, 'blk', 0, 0, tiled=True)  7.3 us
    pallas_call x1, Pallas kernels, band_step(): pl.pallas_call(lambda *refs: band_kernel(*refs, cycles=cycles, order_coun...  6.97 us
    all_gather x1, blocking collectives, shards(): gathered = lax.all_gather(spectra, 'mblk', axis=0)  5.78 us
    convert_element_type x1, local copies, waits for them, and re-layouts, shards(): return (jnp.transpose(result, (1, 0, 2)) * scale_factor).astype(bf16)  1.94 us
  transfers between devices with their start and end apart: 1, of which 1 were waited for; matrix products, arithmetic and copies ran while one was open for 0% of the time, Pallas kernels for 0%

profile of v1, /device:TPU:0, one launch (start us, length us, event | category | flops | bytes accessed | tf_op | source)
XLA Modules:
  0.0 79.7 jit_solution(5786666913757189810)
XLA Ops:
  0.0 0.0 copy-start.5
  0.0 0.0 copy-start.6
  0.0 0.0 copy-start
  0.0 0.0 copy-start.3
  0.0 0.0 copy-start.4
  0.0 18.6 %fusion.6 = bf16[40,6,512]{0,1,2:T(8,128)(2,1)S(1)} fusion(bf16[512,40,1024]{2,1,0:T(8,128)(2,1)} %param.10, bf16[6,512,1024]{2,1,0:T(8,128)(2,1)} %bitcast.15), kind=kOutput, calls=%fused_computation.5 | convolution fusion | flops 251781120 | bytes 48480256 | tf_op jit(solution)/shard_map/dot_general | solution.py:158
  18.6 1.0 %copy.18 = bf16[40,6,512]{2,1,0:T(8,128)(2,1)S(1)} copy(bf16[40,6,512]{0,1,2:T(8,128)(2,1)S(1)} %fusion.6) | data formatting | bytes 491520 | tf_op jit(solution)/shard_map/convert_element_type | solution.py:161
  19.6 0.8 convert_element_type.20
  20.4 7.3 %all-to-all-start = ((bf16[8,30,512]{2,1,0:T(8,128)(2,1)}), bf16[8,30,512]{2,1,0:T(8,128)(2,1)S(1)}, u32[]{:S(2)}, u32[]{:S(2)}) async-start(bf16[8,30,512]{2,1,0:T(8,128)(2,1)} %convert_element_type.20), calls=%async_computation | async-start | bytes 524288 | tf_op jit(solution)/shard_map/all_to_all | solution.py:162
  27.7 0.0 copy-done.5
  27.7 0.1 dynamic_slice.3
  27.8 0.0 copy-done.6
  27.8 8.8 %all-to-all-done = bf16[8,30,512]{2,1,0:T(8,128)(2,1)S(1)} async-done(((bf16[8,30,512]{2,1,0:T(8,128)(2,1)}), bf16[8,30,512]{2,1,0:T(8,128)(2,1)S(1)}, u32[]{:S(2)}, u32[]{:S(2)}) %all-to-all-start) | async-done | bytes 245792 | tf_op jit(solution)/shard_map/all_to_all | solution.py:162
  36.7 5.8 %all-gather.1.refs_0_ = f32[4,30,512]{2,1,0:T(8,128)S(1)} all-gather(f32[1,30,512]{2,1,0:T(8,128)S(1)} %bitcast.16), channel_id=2, replica_groups=mesh['blk'=8,'mblk'=4] {'mblk'}, dimensions={0}, use_global_device_ids=true | all-gather | bytes 307200 | tf_op jit(solution)/shard_map/all_gather | solution.py:164
  42.5 0.0 copy-done
  42.5 0.0 copy-done.1
  42.5 0.0 copy-done.2
  42.5 0.0 copy-done.3
  42.5 0.0 copy-done.4
  42.5 7.0 %band.1 = bf16[8,10,512]{2,1,0:T(8,128)(2,1)S(1)} custom-call(f32[4,30,512]{2,1,0:T(8,128)S(1)} %all-gather.1.refs_0_, s32[1,2048]{1,0:T(1,128)S(1)} %bitcast.13, s32[1,512]{1,0:T(1,128)S(1)} %bitcast.14, f32[1,5]{1,0:T(1,128)S(1)} %multiply_bitcast_fusion.refs_3_, bf16[128,96]{1,0:T(8,128)(2,1)S(1)} %copy-done.3, bf16[768,128]{1,0:T(8,128)(2,1)S(1)} %copy-done.1, ...), custom_call_target="tpu_custom_call" | custom-call | tf_op jit(solution)/shard_map/band/pallas_call | solution.py:140
  49.5 10.9 %all_to_all.10 = bf16[8,10,512]{2,1,0:T(8,128)(2,1)S(1)} all-to-all(bf16[8,10,512]{2,1,0:T(8,128)(2,1)S(1)} %band.1), channel_id=1, replica_groups=mesh['blk'=8,'mblk'=4] {'blk'}, dimensions={0} | all-to-all | bytes 163840 | tf_op jit(solution)/shard_map/all_to_all | solution.py:167
  60.4 0.2 copy.19
  60.6 17.2 %fusion.2 = bf16[2,512,1024]{2,0,1:T(2,128)(2,1)S(1)} fusion(bf16[40,2,512]{0,1,2:T(2,128)(2,1)S(1)} %copy.19, bf16[512,40,1024]{2,1,0:T(8,128)(2,1)} %param.10), kind=kOutput, calls=%fused_computation.3 | convolution fusion | flops 85983232 | bytes 44122112 | tf_op jit(solution)/shard_map/dot_general | solution.py:168
  77.8 1.9 %copy.20 = bf16[2,512,1024]{2,1,0:T(8,128)(2,1)} copy(bf16[2,512,1024]{2,0,1:T(2,128)(2,1)S(1)} %fusion.2) | data formatting | bytes 4194304 | tf_op jit(solution)/shard_map/convert_element_type | solution.py:175
  (5 shorter events, 0.1 us)
Async XLA Ops:
  0.0 27.7 %copy-start.5 = (s32[2048]{0:T(1024)S(1)}, s32[2048]{0:T(1024)}, u32[]{:S(2)}) copy-start(s32[2048]{0:T(1024)} %param.11) | copy-start | bytes 24580
  0.0 27.8 %copy-start.6 = (f32[5]{0:T(128)S(1)}, f32[5]{0:T(128)}, u32[]{:S(2)}) copy-start(f32[5]{0:T(128)} %param.12) | copy-start | bytes 64
  0.0 42.5 %copy-start = (bf16[384,256]{1,0:T(8,128)(2,1)S(1)}, bf16[384,256]{1,0:T(8,128)(2,1)}, u32[]{:S(2)}) copy-start(bf16[384,256]{1,0:T(8,128)(2,1)} %constant.28.clone.refs_6_) | copy-start | bytes 589828
  0.0 42.5 %copy-start.1 = (bf16[768,128]{1,0:T(8,128)(2,1)S(1)}, bf16[768,128]{1,0:T(8,128)(2,1)}, u32[]{:S(2)}) copy-start(bf16[768,128]{1,0:T(8,128)(2,1)} %constant.27.clone.refs_5_) | copy-start | bytes 589828
  0.0 42.5 %copy-start.2 = (f32[2,64,128]{2,1,0:T(8,128)S(1)}, f32[2,64,128]{2,1,0:T(8,128)}, u32[]{:S(2)}) copy-start(f32[2,64,128]{2,1,0:T(8,128)} %constant.30.clone.refs_8_) | copy-start | bytes 196612
  0.0 42.5 %copy-start.3 = (bf16[128,96]{1,0:T(8,128)(2,1)S(1)}, bf16[128,96]{1,0:T(8,128)(2,1)}, u32[]{:S(2)}) copy-start(bf16[128,96]{1,0:T(8,128)(2,1)} %constant.26.clone.refs_4_) | copy-start | bytes 73732
  0.0 42.4 %copy-start.4 = (bf16[32,384]{1,0:T(8,128)(2,1)S(1)}, bf16[32,384]{1,0:T(8,128)(2,1)}, u32[]{:S(2)}) copy-start(bf16[32,384]{1,0:T(8,128)(2,1)} %constant.29.clone.refs_7_) | copy-start | bytes 73732
  20.4 16.2 %all-to-all-start = ((bf16[8,30,512]{2,1,0:T(8,128)(2,1)}), bf16[8,30,512]{2,1,0:T(8,128)(2,1)S(1)}, u32[]{:S(2)}, u32[]{:S(2)}) async-start(bf16[8,30,512]{2,1,0:T(8,128)(2,1)} %convert_element_type.20), calls=%async_computation | async-start | bytes 524288 | tf_op jit(solution)/shard_map/all_to_all | solution.py:162

commit v2 on v1

v2 whole, which is shorter than its diff:
```python
import math

import jax
import jax.numpy as jnp
import numpy as np
from jax import lax
from jax.experimental import pallas as pl
from jax.experimental.pallas import tpu as pltpu
from jax.sharding import PartitionSpec as P

NPHI = 32768
LANES = 128

f32 = jnp.float32
bf16 = jnp.bfloat16


def grid_size(order_count):
    size = LANES
    while size <= 4 * (order_count - 1):
        size *= 2
    return min(size, NPHI)


def split_np(table):
    high = table.astype(jnp.bfloat16)
    low = (table - high.astype(np.float64)).astype(jnp.bfloat16)
    return high, low


def fourier_tables(order_count):
    size = grid_size(order_count)
    n2 = LANES
    n1 = size // n2
    k1 = order_count // n2
    turn = 2.0 * np.pi
    ang1 = turn * (np.outer(np.arange(n1), np.arange(k1)) % n1) / n1
    c1, s1 = np.cos(ang1), np.sin(ang1)
    ang2 = turn * (np.outer(np.arange(n2), np.arange(n2)) % n2) / n2
    c2, s2 = np.cos(ang2), np.sin(ang2)
    angt = turn * np.outer(np.arange(n1), np.arange(n2)) / size
    first = np.block([[c1, -s1], [s1, c1]])
    second = np.concatenate([c2, -s2], axis=0)
    third = np.concatenate([c2, -s2], axis=1)
    fourth = np.block([[c1.T, s1.T], [-s1.T, c1.T]])
    h, l = split_np(first)
    first3 = np.concatenate([h, h, l], axis=1)
    h, l = split_np(second)
    second3 = np.concatenate([h, h, l], axis=0)
    h, l = split_np(third)
    third3 = np.concatenate([h, h, l], axis=0)
    h, l = split_np(fourth)
    fourth3 = np.concatenate([h, h, l], axis=1)
    twiddle = np.stack([np.cos(angt), np.sin(angt)]).astype(np.float32)
    return first3, second3, third3, fourth3, twiddle


def split2(value):
    high = value.astype(bf16)
    low = (value - high.astype(f32)).astype(bf16)
    return high, low


def mm(a, b):
    return jnp.dot(a, b, preferred_element_type=f32)


def band_kernel(
    place_ref, spec_ref, order_ref, weight_ref, first_ref, second_ref, third_ref, fourth_ref, twid_ref,
    out_ref, high_ref, low_ref, line_ref, *, order_count, copies,
):
    blocks, rows, width = spec_ref.shape
    cycles = rows // 6
    n2 = LANES
    k1 = order_count // n2
    n1 = twid_ref.shape[1]
    orders = order_ref[...]
    mask1 = lax.broadcasted_iota(jnp.int32, (k1, order_count), 0) == orders // n2
    mask1 = jnp.where(mask1, 1.0, 0.0).astype(bf16)
    hot2 = lax.broadcasted_iota(jnp.int32, (n2, order_count), 0) == orders % n2
    hot2 = jnp.where(hot2, 1.0, 0.0).astype(bf16)
    for block in range(blocks):
        lanes = slice(block * width, (block + 1) * width)
        value = spec_ref[block]
        low = value - value.astype(bf16).astype(f32)
        line_ref[...] = low
        for row in range(rows):
            span = slice(row * k1, (row + 1) * k1)
            high_ref[span, lanes] = (
                jnp.broadcast_to(spec_ref[block, row : row + 1, :], (k1, width)).astype(bf16) * mask1[:, lanes]
            )
            low_ref[span, lanes] = (
                jnp.broadcast_to(line_ref[row : row + 1, :], (k1, width)).astype(bf16) * mask1[:, lanes]
            )
    contract = (((1,), (1,)), ((), ()))
    ordered = lax.dot_general(high_ref[...], hot2, contract, preferred_element_type=f32)
    ordered = ordered + lax.dot_general(low_ref[...], hot2, contract, preferred_element_type=f32)
    cosine = twid_ref[0]
    sine = twid_ref[1]
    scale = 1.0 / math.sqrt(order_count)
    columns = []
    for cycle in range(cycles):
        for field in range(3):
            first_row = (2 * field * cycles + cycle) * k1
            second_row = first_row + cycles * k1
            columns.append(
                jnp.concatenate(
                    [ordered[first_row : first_row + k1, :], ordered[second_row : second_row + k1, :]], axis=0
                )
            )
    high, low = split2(jnp.concatenate(columns, axis=1))
    part = mm(first_ref[...], jnp.concatenate([high, low, high], axis=0))
    turned = []
    for column in range(3 * cycles):
        lanes = slice(column * n2, (column + 1) * n2)
        re, im = part[:n1, lanes], part[n1:, lanes]
        turned.append(jnp.concatenate([re * cosine - im * sine, re * sine + im * cosine], axis=1))
    high, low = split2(jnp.concatenate(turned, axis=0))
    maps = mm(jnp.concatenate([high, low, high], axis=1), second_ref[...]) * scale
    products = []
    for cycle in range(cycles):
        start = 3 * cycle * n1
        product = maps[start : start + n1] * maps[start + n1 : start + 2 * n1]
        products.append(product * maps[start + 2 * n1 : start + 3 * n1])
    high, low = split2(jnp.concatenate(products, axis=0))
    part = mm(jnp.concatenate([high, low, high], axis=1), third_ref[...])
    turned = []
    for cycle in range(cycles):
        re, im = part[cycle * n1 : (cycle + 1) * n1, :n2], part[cycle * n1 : (cycle + 1) * n1, n2:]
        turned.append(jnp.concatenate([re * cosine + im * sine, im * cosine - re * sine], axis=0))
    high, low = split2(jnp.concatenate(turned, axis=1))
    sums = mm(fourth_ref[...], jnp.concatenate([high, low, high], axis=0))
    factor = NPHI / (n1 * n2) / math.sqrt(NPHI)
    results = [
        sums[:, cycle * n2 : (cycle + 1) * n2] * (weight_ref[0, cycle] * factor) for cycle in range(cycles)
    ]
    high, low = split2(jnp.concatenate(results, axis=0))
    own = order_ref[:, pl.ds(place_ref[0] * width, width)]
    own1 = lax.broadcasted_iota(jnp.int32, (k1, width), 0) == own // n2
    own2 = lax.broadcasted_iota(jnp.int32, (n2, width), 0) == own % n2
    own2 = jnp.where(own2, 1.0, 0.0).astype(bf16)
    picked = mm(jnp.concatenate([high, low], axis=1), jnp.concatenate([own2, own2], axis=0))
    parts = []
    for part in range(2):
        for cycle in range(cycles):
            row = (2 * cycle + part) * k1
            chosen = jnp.where(own1, picked[row : row + k1, :], 0.0)
            parts.append(jnp.sum(chosen, axis=0, keepdims=True))
    weighted = jnp.concatenate(parts, axis=0).astype(bf16)
    for copy in range(copies):
        out_ref[copy] = weighted


def band_step(place, spectra, orders, weights, copies):
    order_count = orders.shape[0]
    tables = fourier_tables(order_count)
    blocks, rows, width = spectra.shape
    k1 = order_count // LANES
    smem = pl.BlockSpec(memory_space=pltpu.SMEM)
    vmem = pl.BlockSpec(memory_space=pltpu.VMEM)
    return pl.pallas_call(
        lambda *refs: band_kernel(*refs, order_count=order_count, copies=copies),
        out_shape=pltpu.VMEM((copies, rows // 3, width), bf16),
        in_specs=[smem, vmem, vmem, smem] + [vmem] * 5,
        out_specs=vmem,
        scratch_shapes=[pltpu.VMEM((rows * k1, order_count), bf16)] * 2 + [pltpu.VMEM((rows, width), f32)],
        compiler_params=pltpu.CompilerParams(vmem_limit_bytes=12 * 2**20),
        name="band",
    )(place, spectra, orders[None, :], weights[None, :], *tables)


CHUNK = 32
GROUP = 16
STEP = 32
AHEAD = 3


def synthesis_kernel(alm_ref, leg_ref, out_ref, keep_ref, alm_buf, acc_ref, row_ref, alm_sem, leg_sem, *, bands):
    fields, m_dev, l_dev = alm_ref.shape
    cycle_count = leg_ref.shape[1]
    cycles = cycle_count // bands
    chunks = m_dev // STEP
    per_tile = LANES // GROUP

    def alm_copy(chunk):
        rows = pl.ds(chunk * STEP, STEP)
        return pltpu.make_async_copy(alm_ref.at[:, rows], alm_buf.at[:, rows], alm_sem.at[chunk])

    def leg_copy(chunk):
        rows = pl.ds(chunk * STEP, STEP)
        return pltpu.make_async_copy(leg_ref.at[rows], keep_ref.at[rows], leg_sem.at[chunk])

    for chunk in range(min(AHEAD, chunks)):
        alm_copy(chunk).start()
        leg_copy(chunk).start()
    width = fields * GROUP
    lane = lax.broadcasted_iota(jnp.int32, (1, width), 1) % GROUP
    tile_lane = lax.broadcasted_iota(jnp.int32, (1, LANES), 1) // GROUP

    def one_tile(tile, carry):
        sums = [None] * fields
        for place in range(per_tile):
            number = tile * per_tile + place
            if place * GROUP % STEP == 0:
                chunk = number * GROUP // STEP

                @pl.when(chunk + AHEAD < chunks)
                def _():
                    alm_copy(chunk + AHEAD).start()
                    leg_copy(chunk + AHEAD).start()

                alm_copy(chunk).wait()
                leg_copy(chunk).wait()
            rows = pl.ds(number * GROUP, GROUP)
            right = alm_buf[:, rows, :].reshape(width, l_dev)
            own = None
            for half in range(2):
                left = keep_ref[pl.ds(number * GROUP + half * GROUP // 2, GROUP // 2)]
                both = lax.dot_general(
                    left.reshape(GROUP // 2 * cycle_count, l_dev),
                    right,
                    (((1,), (1,)), ((), ())),
                    preferred_element_type=f32,
                )
                for order in range(GROUP // 2):
                    part = both[order * cycle_count : (order + 1) * cycle_count]
                    part = jnp.where(lane == half * GROUP // 2 + order, part, 0.0)
                    own = part if own is None else own + part
            own = jnp.concatenate([own, jnp.zeros((cycle_count, LANES - width), f32)], axis=1)
            for field in range(fields):
                shift = (place - field) * GROUP % LANES
                moved = pltpu.roll(own, shift, 1) if shift else own
                moved = jnp.where(tile_lane == place, moved, 0.0)
                sums[field] = moved if sums[field] is None else sums[field] + moved
        for field in range(fields):
            acc_ref[tile, field] = sums[field]
        return carry

    lax.fori_loop(0, m_dev // LANES, one_tile, 0)
    for tile in range(m_dev // LANES):
        lanes = slice(tile * LANES, (tile + 1) * LANES)
        for band in range(bands):
            for field in range(fields):
                row_ref[band, field * cycles : (field + 1) * cycles, lanes] = acc_ref[
                    tile, field, band * cycles : (band + 1) * cycles, :
                ]
    out_ref[...] = row_ref[...].astype(bf16)


def synthesis(coeffs, legendre, bands):
    fields, m_dev, l_dev = coeffs.shape
    cycle_count = legendre.shape[1]
    rows = fields * cycle_count // bands
    chunks = m_dev // STEP
    hbm = pl.BlockSpec(memory_space=pl.ANY)
    vmem = pl.BlockSpec(memory_space=pltpu.VMEM)
    return pl.pallas_call(
        lambda *refs: synthesis_kernel(*refs, bands=bands),
        out_shape=[
            jax.ShapeDtypeStruct((bands, rows, m_dev), bf16),
            pltpu.VMEM(legendre.shape, bf16),
        ],
        in_specs=[hbm, hbm],
        out_specs=[vmem, vmem],
        scratch_shapes=[
            pltpu.VMEM(coeffs.shape, bf16),
            pltpu.VMEM((m_dev // LANES, fields, cycle_count, LANES), f32),
            pltpu.VMEM((bands, rows, m_dev), f32),
            pltpu.SemaphoreType.DMA((chunks,)),
            pltpu.SemaphoreType.DMA((chunks,)),
        ],
        compiler_params=pltpu.CompilerParams(vmem_limit_bytes=14 * 2**20),
        name="synthesis",
    )(
        pltpu.with_memory_space_constraint(coeffs, pltpu.HBM),
        pltpu.with_memory_space_constraint(legendre, pltpu.HBM),
    )


def analysis_kernel(weighted_ref, keep_ref, out_ref, rows_ref, wide_ref, buf_ref, sem, *, scale):
    bands, part_rows, m_dev = weighted_ref.shape
    cycles = part_rows // 2
    cycle_count, l_dev = keep_ref.shape[1:]
    width = CHUNK * cycle_count
    spread = lax.broadcasted_iota(jnp.int32, (cycle_count, width), 1) % cycle_count
    spread = (spread == lax.broadcasted_iota(jnp.int32, (cycle_count, width), 0)).astype(f32).astype(bf16)
    for part in range(2):
        for band in range(bands):
            rows_ref[part, band * cycles : (band + 1) * cycles, :] = weighted_ref[
                band, part * cycles : (part + 1) * cycles, :
            ].astype(f32)
        wide_ref[part] = rows_ref[part].T.astype(bf16)
    diagonal = lax.broadcasted_iota(jnp.int32, (CHUNK, width), 1) // cycle_count
    diagonal = diagonal == lax.broadcasted_iota(jnp.int32, (CHUNK, width), 0)

    def out_copy(chunk, slot):
        return pltpu.make_async_copy(
            buf_ref.at[slot], out_ref.at[:, pl.ds(chunk * CHUNK, CHUNK)], sem.at[slot]
        )

    def one_chunk(chunk, carry):
        slot = chunk % 2
        rows = pl.ds(chunk * CHUNK, CHUNK)
        parts = [
            jnp.where(diagonal, mm(wide_ref[part, rows, :], spread), 0.0).astype(bf16) for part in range(2)
        ]
        left = jnp.concatenate(parts, axis=0)
        right = keep_ref[rows].reshape(width, l_dev)
        result = mm(left, right) * scale

        @pl.when(chunk >= 2)
        def _():
            out_copy(chunk - 2, slot).wait()

        buf_ref[slot] = result.reshape(2, CHUNK, l_dev).astype(bf16)
        out_copy(chunk, slot).start()
        return carry

    chunks = m_dev // CHUNK
    lax.fori_loop(0, chunks, one_chunk, 0)
    for chunk in range(max(chunks - 2, 0), chunks):
        out_copy(chunk, chunk % 2).wait()


def analysis(weighted, keep, scale):
    m_dev, cycle_count, l_dev = keep.shape
    vmem = pl.BlockSpec(memory_space=pltpu.VMEM)
    return pl.pallas_call(
        lambda *refs: analysis_kernel(*refs, scale=scale),
        out_shape=jax.ShapeDtypeStruct((2, m_dev, l_dev), bf16),
        in_specs=[vmem, vmem],
        out_specs=pl.BlockSpec(memory_space=pl.ANY),
        scratch_shapes=[
            pltpu.VMEM((2, cycle_count, m_dev), f32),
            pltpu.VMEM((2, m_dev, cycle_count), bf16),
            pltpu.VMEM((2, 2, CHUNK, l_dev), bf16),
            pltpu.SemaphoreType.DMA((2,)),
        ],
        compiler_params=pltpu.CompilerParams(vmem_limit_bytes=14 * 2**20),
        name="analysis",
    )(
        pltpu.with_memory_space_constraint(weighted, pltpu.VMEM),
        pltpu.with_memory_space_constraint(keep, pltpu.VMEM),
    )


def shards(alm, legendre, m_value, cycle_weight):
    m_dev, cycle_count, l_dev = legendre.shape
    bands = lax.axis_size("blk")
    place = lax.axis_index("mblk").astype(jnp.int32)[None]
    outgoing, keep = synthesis(alm.reshape(6, m_dev, l_dev), legendre, bands)
    outgoing, place, cycle_weight = lax.optimization_barrier((outgoing, place, cycle_weight))
    incoming = lax.all_to_all(outgoing, "blk", 0, 0, tiled=True)
    spectra = jnp.sum(incoming.astype(f32), axis=0)
    gathered = lax.all_gather(spectra, "mblk", axis=0)
    copies = band_step(place, gathered, m_value, cycle_weight, bands)
    weighted = lax.all_to_all(copies, "blk", 0, 0, tiled=True)
    return analysis(weighted, keep, math.sqrt(l_dev * bands / cycle_count))


def solution(mesh):
    in_specs = (P(None, None, "mblk", "blk"), P("mblk", None, "blk"), P(), P("blk"))
    out_specs = P(None, "mblk", "blk")
    return jax.shard_map(shards, mesh=mesh, in_specs=in_specs, out_specs=out_specs, check_vma=False)
```

time: 80 us -> 67.4 us (0.84)
  matrix products: 35.7 us -> 0 us
  Pallas kernels: 6.97 us -> 34.1 us
  blocking collectives: 16.7 us -> 32.9 us
  waiting for transfers between devices: 8.83 us -> 0 us
  starting transfers between devices: 7.3 us -> 0 us
  local copies, waits for them, and re-layouts: 4.09 us -> 0.03 us
    dot_general x2 -> x0, matrix products: 35.7 us -> none  [the longest x1 18.6 us: shards(): lax.dot_general(coeffs, legendre, (((2,), (2,)), ((1,), (0,))), preferred...]
    pallas_call x1 -> x3, Pallas kernels: 6.97 us -> 34.1 us  [the longest x1 18 us: synthesis(): pl.pallas_call(lambda *refs: synthesis_kernel(*refs, bands=bands), out_sh...]
    all_to_all x0 -> x1, blocking collectives: none -> 16.2 us  [shards(): incoming = lax.all_to_all(outgoing, 'blk', 0, 0, tiled=True)]
    all_to_all x1 -> x0, waiting for transfers between devices: 8.83 us -> none  [shards(): incoming = lax.all_to_all(outgoing, 'blk', 0, 0, tiled=True)]
    all_to_all x1 -> x0, starting transfers between devices: 7.3 us -> none  [shards(): incoming = lax.all_to_all(outgoing, 'blk', 0, 0, tiled=True)]
    convert_element_type x3 -> x0, local copies, waits for them, and re-layouts: 3.75 us -> none  [the longest x1 1.94 us: shards(): return (jnp.transpose(result, (1, 0, 2)) * scale_factor).astype(bf16)]
  transfers between devices with their start and end apart: 1 -> 0, of which waited for: 1 -> 0; matrix products, arithmetic and copies ran while one was open for 0% -> 0% of each run, Pallas kernels for 0% -> 0%
where the time goes in v2:
time: 67.4 us; the launch traced here: 67.2 us
  Pallas kernels  34.1 us (51%)
  blocking collectives  32.9 us (49%)
    pallas_call x1, Pallas kernels, synthesis(): pl.pallas_call(lambda *refs: synthesis_kernel(*refs, bands=bands), out_sh...  18 us
    all_to_all x1, blocking collectives, shards(): incoming = lax.all_to_all(outgoing, 'blk', 0, 0, tiled=True)  16.2 us
    pallas_call x1, Pallas kernels, analysis(): pl.pallas_call(lambda *refs: analysis_kernel(*refs, scale=scale), out_sha...  12 us
    all_to_all x1, blocking collectives, shards(): weighted = lax.all_to_all(copies, 'blk', 0, 0, tiled=True)  10.9 us
    all_gather x1, blocking collectives, shards(): gathered = lax.all_gather(spectra, 'mblk', axis=0)  5.78 us
    pallas_call x1, Pallas kernels, band_step(): pl.pallas_call(lambda *refs: band_kernel(*refs, order_count=order_count,...  4.12 us

profile of v2, /device:TPU:0, one launch (start us, length us, event | category | flops | bytes accessed | tf_op | source)
XLA Modules:
  0.0 67.2 jit_solution(5885861017732075845)
XLA Ops:
  0.0 0.0 copy-start.2
  0.0 0.0 copy-start.4
  0.0 0.0 copy-start
  0.0 0.0 copy-start.1
  0.0 0.0 copy-start.3
  0.0 0.0 copy-start.6
  0.0 0.0 copy-start.5
  0.0 18.0 %synthesis.1 = (bf16[8,30,512]{2,1,0:T(8,128)(2,1)}, bf16[512,40,1024]{2,1,0:T(8,128)(2,1)S(1)}) custom-call(bf16[6,512,1024]{2,1,0:T(8,128)(2,1)} %bitcast.7, bf16[512,40,1024]{2,1,0:T(8,128)(2,1)} %refs_1_.1), custom_call_target="tpu_custom_call" | custom-call | tf_op jit(solution)/shard_map/synthesis/pallas_call | solution.py:257
  18.0 16.2 %all_to_all.10 = bf16[8,30,512]{2,1,0:T(8,128)(2,1)S(1)} all-to-all(bf16[8,30,512]{2,1,0:T(8,128)(2,1)} %get-tuple-element.12), channel_id=1, replica_groups=mesh['blk'=8,'mblk'=4] {'blk'}, dimensions={0} | all-to-all | bytes 491520 | tf_op jit(solution)/shard_map/all_to_all | solution.py:353
  34.3 5.8 %all-gather.1.refs_1_ = f32[4,30,512]{2,1,0:T(8,128)S(1)} all-gather(f32[1,30,512]{2,1,0:T(8,128)S(1)} %bitcast.8), channel_id=2, replica_groups=mesh['blk'=8,'mblk'=4] {'mblk'}, dimensions={0}, use_global_device_ids=true | all-gather | bytes 307200 | tf_op jit(solution)/shard_map/all_gather | solution.py:355
  40.1 0.0 copy-done.2
  40.1 0.0 copy-done.4
  40.1 0.0 copy-done
  40.1 0.0 copy-done.1
  40.1 0.0 copy-done.3
  40.1 0.0 copy-done.6
  40.1 0.0 copy-done.5
  40.1 4.1 %band.1 = bf16[8,10,512]{2,1,0:T(8,128)(2,1)S(1)} custom-call(s32[1]{0:T(128)} %bitcast.1.refs_0_, f32[4,30,512]{2,1,0:T(8,128)S(1)} %all-gather.1.refs_1_, s32[1,2048]{1,0:T(1,128)S(1)} %bitcast.5, f32[1,5]{1,0:T(1,128)S(1)} %bitcast.6, bf16[128,96]{1,0:T(8,128)(2,1)S(1)} %copy-done.3, bf16[768,128]{1,0:T(8,128)(2,1)S(1)} %copy-done.1, ...), custom_call_target="tpu_custom_call" | custom-call | tf_op jit(solution)/shard_map/band/pallas_call | solution.py:161
  44.3 10.9 %all_to_all.11.refs_0_ = bf16[8,10,512]{2,1,0:T(8,128)(2,1)S(1)} all-to-all(bf16[8,10,512]{2,1,0:T(8,128)(2,1)S(1)} %band.1), channel_id=1, replica_groups=mesh['blk'=8,'mblk'=4] {'blk'}, dimensions={0} | all-to-all | bytes 163840 | tf_op jit(solution)/shard_map/all_to_all | solution.py:357
  55.1 12.0 %analysis.1 = bf16[2,512,1024]{2,1,0:T(8,128)(2,1)} custom-call(bf16[8,10,512]{2,1,0:T(8,128)(2,1)S(1)} %all_to_all.11.refs_0_, bf16[512,40,1024]{2,1,0:T(8,128)(2,1)S(1)} %get-tuple-element.14.refs_1_), custom_call_target="tpu_custom_call" | custom-call | tf_op jit(solution)/shard_map/analysis/pallas_call | solution.py:328
  (1 shorter events, 0.0 us)
Async XLA Ops:
  0.0 40.1 %copy-start.2 = (f32[2,64,128]{2,1,0:T(8,128)S(1)}, f32[2,64,128]{2,1,0:T(8,128)}, u32[]{:S(2)}) copy-start(f32[2,64,128]{2,1,0:T(8,128)} %constant.20.clone.refs_8_) | copy-start | bytes 196612
  0.0 40.1 %copy-start.4 = (bf16[32,384]{1,0:T(8,128)(2,1)S(1)}, bf16[32,384]{1,0:T(8,128)(2,1)}, u32[]{:S(2)}) copy-start(bf16[32,384]{1,0:T(8,128)(2,1)} %constant.19.clone.refs_7_) | copy-start | bytes 73732
  0.0 40.1 %copy-start = (bf16[384,256]{1,0:T(8,128)(2,1)S(1)}, bf16[384,256]{1,0:T(8,128)(2,1)}, u32[]{:S(2)}) copy-start(bf16[384,256]{1,0:T(8,128)(2,1)} %constant.18.clone.refs_6_) | copy-start | bytes 589828
  0.0 40.1 %copy-start.1 = (bf16[768,128]{1,0:T(8,128)(2,1)S(1)}, bf16[768,128]{1,0:T(8,128)(2,1)}, u32[]{:S(2)}) copy-start(bf16[768,128]{1,0:T(8,128)(2,1)} %constant.17.clone.refs_5_) | copy-start | bytes 589828
  0.0 40.1 %copy-start.3 = (bf16[128,96]{1,0:T(8,128)(2,1)S(1)}, bf16[128,96]{1,0:T(8,128)(2,1)}, u32[]{:S(2)}) copy-start(bf16[128,96]{1,0:T(8,128)(2,1)} %constant.16.clone.refs_4_) | copy-start | bytes 73732
  0.0 40.1 %copy-start.6 = (f32[5]{0:T(128)S(1)}, f32[5]{0:T(128)}, u32[]{:S(2)}) copy-start(f32[5]{0:T(128)} %param.12) | copy-start | bytes 64
  0.0 40.1 %copy-start.5 = (s32[2048]{0:T(1024)S(1)}, s32[2048]{0:T(1024)}, u32[]{:S(2)}) copy-start(s32[2048]{0:T(1024)} %param.11) | copy-start | bytes 24580

commit v3 on v2

--- a/solution.py
+++ b/solution.py
@@ -63,6 +63,14 @@
 
 def mm(a, b):
     return jnp.dot(a, b, preferred_element_type=f32)
+
+
+def mm_pieces(a, b):
+    total = None
+    for first in range(0, a.shape[1], LANES):
+        part = mm(a[:, first : first + LANES], b[first : first + LANES])
+        total = part if total is None else total + part
+    return total
 
 
 def band_kernel(
@@ -171,6 +179,7 @@
 
 CHUNK = 32
 GROUP = 16
+PAIR = 4
 STEP = 32
 AHEAD = 3
 
@@ -277,54 +286,64 @@
     )
 
 
-def analysis_kernel(weighted_ref, keep_ref, out_ref, rows_ref, wide_ref, buf_ref, sem, *, scale):
+def analysis_kernel(weighted_ref, keep_ref, out_ref, rows_ref, wide_ref, left_ref, buf_ref, sem, *, scale):
     bands, part_rows, m_dev = weighted_ref.shape
     cycles = part_rows // 2
     cycle_count, l_dev = keep_ref.shape[1:]
     width = CHUNK * cycle_count
+    pair = left_ref.shape[1]
+    chunks = m_dev // CHUNK
+    steps = chunks // pair
     spread = lax.broadcasted_iota(jnp.int32, (cycle_count, width), 1) % cycle_count
-    spread = (spread == lax.broadcasted_iota(jnp.int32, (cycle_count, width), 0)).astype(f32).astype(bf16)
+    spread = spread == lax.broadcasted_iota(jnp.int32, (cycle_count, width), 0)
+    spread = jnp.where(spread, 1.0, 0.0).astype(bf16)
     for part in range(2):
         for band in range(bands):
             rows_ref[part, band * cycles : (band + 1) * cycles, :] = weighted_ref[
                 band, part * cycles : (part + 1) * cycles, :
             ].astype(f32)
-        wide_ref[part] = rows_ref[part].T.astype(bf16)
+        wide_ref[:, part] = rows_ref[part].T.astype(bf16).reshape(chunks, CHUNK, cycle_count)
     diagonal = lax.broadcasted_iota(jnp.int32, (CHUNK, width), 1) // cycle_count
     diagonal = diagonal == lax.broadcasted_iota(jnp.int32, (CHUNK, width), 0)
 
-    def out_copy(chunk, slot):
-        return pltpu.make_async_copy(
-            buf_ref.at[slot], out_ref.at[:, pl.ds(chunk * CHUNK, CHUNK)], sem.at[slot]
-        )
-
-    def one_chunk(chunk, carry):
-        slot = chunk % 2
-        rows = pl.ds(chunk * CHUNK, CHUNK)
-        parts = [
-            jnp.where(diagonal, mm(wide_ref[part, rows, :], spread), 0.0).astype(bf16) for part in range(2)
-        ]
-        left = jnp.concatenate(parts, axis=0)
-        right = keep_ref[rows].reshape(width, l_dev)
-        result = mm(left, right) * scale
-
-        @pl.when(chunk >= 2)
+    def build(step, slot):
+        source = wide_ref[pl.ds(step * pair, pair)].reshape(pair * 2 * CHUNK, cycle_count)
+        tiled = mm(source, spread).reshape(pair, 2, CHUNK, width)
+        chosen = jnp.where(diagonal, tiled, 0.0).astype(bf16)
+        left_ref[slot] = chosen.reshape(pair, 2 * CHUNK, width)
+
+    def out_copy(step, slot):
+        rows = pl.ds(step * pair * CHUNK, pair * CHUNK)
+        return pltpu.make_async_copy(buf_ref.at[slot], out_ref.at[:, rows], sem.at[slot])
+
+    build(0, 0)
+
+    def one_step(step, carry):
+        slot = step % 2
+
+        @pl.when(step >= 2)
         def _():
-            out_copy(chunk - 2, slot).wait()
-
-        buf_ref[slot] = result.reshape(2, CHUNK, l_dev).astype(bf16)
-        out_copy(chunk, slot).start()
+            out_copy(step - 2, slot).wait()
+
+        for item in range(pair):
+            rows = pl.ds((step * pair + item) * CHUNK, CHUNK)
+            right = keep_ref[rows].reshape(width, l_dev)
+            result = mm_pieces(left_ref[slot, item], right) * scale
+            buf_ref[slot, :, item * CHUNK : (item + 1) * CHUNK, :] = result.reshape(2, CHUNK, l_dev).astype(bf16)
+        build(jnp.minimum(step + 1, steps - 1), 1 - slot)
+        out_copy(step, slot).start()
         return carry
 
-    chunks = m_dev // CHUNK
-    lax.fori_loop(0, chunks, one_chunk, 0)
-    for chunk in range(max(chunks - 2, 0), chunks):
-        out_copy(chunk, chunk % 2).wait()
+    lax.fori_loop(0, steps, one_step, 0)
+    for step in range(max(steps - 2, 0), steps):
+        out_copy(step, step % 2).wait()
 
 
 def analysis(weighted, keep, scale):
     m_dev, cycle_count, l_dev = keep.shape
     vmem = pl.BlockSpec(memory_space=pltpu.VMEM)
+    chunks = m_dev // CHUNK
+    pair = math.gcd(chunks, PAIR)
     return pl.pallas_call(
         lambda *refs: analysis_kernel(*refs, scale=scale),
         out_shape=jax.ShapeDtypeStruct((2, m_dev, l_dev), bf16),
@@ -332,8 +351,9 @@
         out_specs=pl.BlockSpec(memory_space=pl.ANY),
         scratch_shapes=[
             pltpu.VMEM((2, cycle_count, m_dev), f32),
-            pltpu.VMEM((2, m_dev, cycle_count), bf16),
-            pltpu.VMEM((2, 2, CHUNK, l_dev), bf16),
+            pltpu.VMEM((chunks, 2, CHUNK, cycle_count), bf16),
+            pltpu.VMEM((2, pair, 2 * CHUNK, CHUNK * cycle_count), bf16),
+            pltpu.VMEM((2, 2, pair * CHUNK, l_dev), bf16),
             pltpu.SemaphoreType.DMA((2,)),
         ],
         compiler_params=pltpu.CompilerParams(vmem_limit_bytes=14 * 2**20),

time: 67.4 us -> 63.2 us (0.938)
  Pallas kernels: 34.1 us -> 29.9 us
    pallas_call x1, Pallas kernels: 12 us -> 7.83 us  [analysis(): pl.pallas_call(lambda *refs: analysis_kernel(*refs, scale=scale), out_sha...]
where the time goes in v3:
time: 63.2 us; the launch traced here: 63 us
  blocking collectives  32.9 us (52%)
  Pallas kernels  29.9 us (47%)
    pallas_call x1, Pallas kernels, synthesis(): pl.pallas_call(lambda *refs: synthesis_kernel(*refs, bands=bands), out_sh...  18 us
    all_to_all x1, blocking collectives, shards(): incoming = lax.all_to_all(outgoing, 'blk', 0, 0, tiled=True)  16.2 us
    all_to_all x1, blocking collectives, shards(): weighted = lax.all_to_all(copies, 'blk', 0, 0, tiled=True)  10.9 us
    pallas_call x1, Pallas kernels, analysis(): pl.pallas_call(lambda *refs: analysis_kernel(*refs, scale=scale), out_sha...  7.83 us
    all_gather x1, blocking collectives, shards(): gathered = lax.all_gather(spectra, 'mblk', axis=0)  5.78 us
    pallas_call x1, Pallas kernels, band_step(): pl.pallas_call(lambda *refs: band_kernel(*refs, order_count=order_count,...  4.12 us

profile of v3, /device:TPU:0, one launch (start us, length us, event | category | flops | bytes accessed | tf_op | source)
XLA Modules:
  0.0 63.0 jit_solution(14082556610930203358)
XLA Ops:
  0.0 0.0 copy-start.2
  0.0 0.0 copy-start.4
  0.0 0.0 copy-start
  0.0 0.0 copy-start.1
  0.0 0.0 copy-start.3
  0.0 0.0 copy-start.6
  0.0 0.0 copy-start.5
  0.0 18.0 %synthesis.1 = (bf16[8,30,512]{2,1,0:T(8,128)(2,1)}, bf16[512,40,1024]{2,1,0:T(8,128)(2,1)S(1)}) custom-call(bf16[6,512,1024]{2,1,0:T(8,128)(2,1)} %bitcast.7, bf16[512,40,1024]{2,1,0:T(8,128)(2,1)} %refs_1_.1), custom_call_target="tpu_custom_call" | custom-call | tf_op jit(solution)/shard_map/synthesis/pallas_call | solution.py:266
  18.0 16.2 %all_to_all.10 = bf16[8,30,512]{2,1,0:T(8,128)(2,1)S(1)} all-to-all(bf16[8,30,512]{2,1,0:T(8,128)(2,1)} %get-tuple-element.12), channel_id=1, replica_groups=mesh['blk'=8,'mblk'=4] {'blk'}, dimensions={0} | all-to-all | bytes 491520 | tf_op jit(solution)/shard_map/all_to_all | solution.py:373
  34.3 5.8 %all-gather.1.refs_1_ = f32[4,30,512]{2,1,0:T(8,128)S(1)} all-gather(f32[1,30,512]{2,1,0:T(8,128)S(1)} %bitcast.8), channel_id=2, replica_groups=mesh['blk'=8,'mblk'=4] {'mblk'}, dimensions={0}, use_global_device_ids=true | all-gather | bytes 307200 | tf_op jit(solution)/shard_map/all_gather | solution.py:375
  40.1 0.0 copy-done.2
  40.1 0.0 copy-done.4
  40.1 0.0 copy-done
  40.1 0.0 copy-done.1
  40.1 0.0 copy-done.3
  40.1 0.0 copy-done.6
  40.1 0.0 copy-done.5
  40.1 4.1 %band.1 = bf16[8,10,512]{2,1,0:T(8,128)(2,1)S(1)} custom-call(s32[1]{0:T(128)} %bitcast.1.refs_0_, f32[4,30,512]{2,1,0:T(8,128)S(1)} %all-gather.1.refs_1_, s32[1,2048]{1,0:T(1,128)S(1)} %bitcast.5, f32[1,5]{1,0:T(1,128)S(1)} %bitcast.6, bf16[128,96]{1,0:T(8,128)(2,1)S(1)} %copy-done.3, bf16[768,128]{1,0:T(8,128)(2,1)S(1)} %copy-done.1, ...), custom_call_target="tpu_custom_call" | custom-call | tf_op jit(solution)/shard_map/band/pallas_call | solution.py:169
  44.3 10.9 %all_to_all.11.refs_0_ = bf16[8,10,512]{2,1,0:T(8,128)(2,1)S(1)} all-to-all(bf16[8,10,512]{2,1,0:T(8,128)(2,1)S(1)} %band.1), channel_id=1, replica_groups=mesh['blk'=8,'mblk'=4] {'blk'}, dimensions={0} | all-to-all | bytes 163840 | tf_op jit(solution)/shard_map/all_to_all | solution.py:377
  55.1 7.8 %analysis.1 = bf16[2,512,1024]{2,1,0:T(8,128)(2,1)} custom-call(bf16[8,10,512]{2,1,0:T(8,128)(2,1)S(1)} %all_to_all.11.refs_0_, bf16[512,40,1024]{2,1,0:T(8,128)(2,1)S(1)} %get-tuple-element.14.refs_1_), custom_call_target="tpu_custom_call" | custom-call | tf_op jit(solution)/shard_map/analysis/pallas_call | solution.py:347
  (1 shorter events, 0.0 us)
Async XLA Ops:
  0.0 40.1 %copy-start.2 = (f32[2,64,128]{2,1,0:T(8,128)S(1)}, f32[2,64,128]{2,1,0:T(8,128)}, u32[]{:S(2)}) copy-start(f32[2,64,128]{2,1,0:T(8,128)} %constant.20.clone.refs_8_) | copy-start | bytes 196612
  0.0 40.1 %copy-start.4 = (bf16[32,384]{1,0:T(8,128)(2,1)S(1)}, bf16[32,384]{1,0:T(8,128)(2,1)}, u32[]{:S(2)}) copy-start(bf16[32,384]{1,0:T(8,128)(2,1)} %constant.19.clone.refs_7_) | copy-start | bytes 73732
  0.0 40.1 %copy-start = (bf16[384,256]{1,0:T(8,128)(2,1)S(1)}, bf16[384,256]{1,0:T(8,128)(2,1)}, u32[]{:S(2)}) copy-start(bf16[384,256]{1,0:T(8,128)(2,1)} %constant.18.clone.refs_6_) | copy-start | bytes 589828
  0.0 40.1 %copy-start.1 = (bf16[768,128]{1,0:T(8,128)(2,1)S(1)}, bf16[768,128]{1,0:T(8,128)(2,1)}, u32[]{:S(2)}) copy-start(bf16[768,128]{1,0:T(8,128)(2,1)} %constant.17.clone.refs_5_) | copy-start | bytes 589828
  0.0 40.1 %copy-start.3 = (bf16[128,96]{1,0:T(8,128)(2,1)S(1)}, bf16[128,96]{1,0:T(8,128)(2,1)}, u32[]{:S(2)}) copy-start(bf16[128,96]{1,0:T(8,128)(2,1)} %constant.16.clone.refs_4_) | copy-start | bytes 73732
  0.0 40.1 %copy-start.6 = (f32[5]{0:T(128)S(1)}, f32[5]{0:T(128)}, u32[]{:S(2)}) copy-start(f32[5]{0:T(128)} %param.12) | copy-start | bytes 64
  0.0 40.1 %copy-start.5 = (s32[2048]{0:T(1024)S(1)}, s32[2048]{0:T(1024)}, u32[]{:S(2)}) copy-start(s32[2048]{0:T(1024)} %param.11) | copy-start | bytes 24580

commit v4 on v3

--- a/solution.py
+++ b/solution.py
@@ -278,7 +278,7 @@
             pltpu.SemaphoreType.DMA((chunks,)),
             pltpu.SemaphoreType.DMA((chunks,)),
         ],
-        compiler_params=pltpu.CompilerParams(vmem_limit_bytes=14 * 2**20),
+        compiler_params=pltpu.CompilerParams(vmem_limit_bytes=11 * 2**20),
         name="synthesis",
     )(
         pltpu.with_memory_space_constraint(coeffs, pltpu.HBM),

time: 63.2 us -> 62.3 us (0.986)
  Pallas kernels: 29.9 us -> 29.2 us
    pallas_call x1, Pallas kernels: 18 us -> 17.3 us  [synthesis(): pl.pallas_call(lambda *refs: synthesis_kernel(*refs, bands=bands), out_sh...]
where the time goes in v4:
time: 62.3 us; the launch traced here: 62.1 us
  blocking collectives  32.7 us (52%)
  Pallas kernels  29.2 us (47%)
    pallas_call x1, Pallas kernels, synthesis(): pl.pallas_call(lambda *refs: synthesis_kernel(*refs, bands=bands), out_sh...  17.3 us
    all_to_all x1, blocking collectives, shards(): incoming = lax.all_to_all(outgoing, 'blk', 0, 0, tiled=True)  16 us
    all_to_all x1, blocking collectives, shards(): weighted = lax.all_to_all(copies, 'blk', 0, 0, tiled=True)  10.9 us
    pallas_call x1, Pallas kernels, analysis(): pl.pallas_call(lambda *refs: analysis_kernel(*refs, scale=scale), out_sha...  7.83 us
    all_gather x1, blocking collectives, shards(): gathered = lax.all_gather(spectra, 'mblk', axis=0)  5.78 us
    pallas_call x1, Pallas kernels, band_step(): pl.pallas_call(lambda *refs: band_kernel(*refs, order_count=order_count,...  4.12 us

profile of v4, /device:TPU:0, one launch (start us, length us, event | category | flops | bytes accessed | tf_op | source)
XLA Modules:
  0.0 62.1 jit_solution(1126976785580607042)
XLA Ops:
  0.0 0.0 copy-start.2
  0.0 0.0 copy-start.4
  0.0 0.0 copy-start
  0.0 0.0 copy-start.1
  0.0 0.0 copy-start.3
  0.0 0.0 copy-start.6
  0.0 0.0 copy-start.5
  0.0 17.3 %synthesis.1 = (bf16[8,30,512]{2,1,0:T(8,128)(2,1)S(1)}, bf16[512,40,1024]{2,1,0:T(8,128)(2,1)S(1)}) custom-call(bf16[6,512,1024]{2,1,0:T(8,128)(2,1)} %bitcast.7, bf16[512,40,1024]{2,1,0:T(8,128)(2,1)} %refs_1_.1), custom_call_target="tpu_custom_call" | custom-call | tf_op jit(solution)/shard_map/synthesis/pallas_call | solution.py:266
  17.3 16.0 %all_to_all.10 = bf16[8,30,512]{2,1,0:T(8,128)(2,1)S(1)} all-to-all(bf16[8,30,512]{2,1,0:T(8,128)(2,1)S(1)} %get-tuple-element.12), channel_id=1, replica_groups=mesh['blk'=8,'mblk'=4] {'blk'}, dimensions={0} | all-to-all | bytes 491520 | tf_op jit(solution)/shard_map/all_to_all | solution.py:373
  33.4 5.8 %all-gather.1.refs_1_ = f32[4,30,512]{2,1,0:T(8,128)S(1)} all-gather(f32[1,30,512]{2,1,0:T(8,128)S(1)} %bitcast.8), channel_id=2, replica_groups=mesh['blk'=8,'mblk'=4] {'mblk'}, dimensions={0}, use_global_device_ids=true | all-gather | bytes 307200 | tf_op jit(solution)/shard_map/all_gather | solution.py:375
  39.2 0.0 copy-done.2
  39.2 0.0 copy-done.4
  39.2 0.0 copy-done
  39.2 0.0 copy-done.1
  39.2 0.0 copy-done.3
  39.2 0.0 copy-done.6
  39.2 0.0 copy-done.5
  39.2 4.1 %band.1 = bf16[8,10,512]{2,1,0:T(8,128)(2,1)S(1)} custom-call(s32[1]{0:T(128)} %bitcast.1.refs_0_, f32[4,30,512]{2,1,0:T(8,128)S(1)} %all-gather.1.refs_1_, s32[1,2048]{1,0:T(1,128)S(1)} %bitcast.5, f32[1,5]{1,0:T(1,128)S(1)} %bitcast.6, bf16[128,96]{1,0:T(8,128)(2,1)S(1)} %copy-done.3, bf16[768,128]{1,0:T(8,128)(2,1)S(1)} %copy-done.1, ...), custom_call_target="tpu_custom_call" | custom-call | tf_op jit(solution)/shard_map/band/pallas_call | solution.py:169
  43.3 10.9 %all_to_all.11.refs_0_ = bf16[8,10,512]{2,1,0:T(8,128)(2,1)S(1)} all-to-all(bf16[8,10,512]{2,1,0:T(8,128)(2,1)S(1)} %band.1), channel_id=1, replica_groups=mesh['blk'=8,'mblk'=4] {'blk'}, dimensions={0} | all-to-all | bytes 163840 | tf_op jit(solution)/shard_map/all_to_all | solution.py:377
  54.2 7.8 %analysis.1 = bf16[2,512,1024]{2,1,0:T(8,128)(2,1)} custom-call(bf16[8,10,512]{2,1,0:T(8,128)(2,1)S(1)} %all_to_all.11.refs_0_, bf16[512,40,1024]{2,1,0:T(8,128)(2,1)S(1)} %get-tuple-element.14.refs_1_), custom_call_target="tpu_custom_call" | custom-call | tf_op jit(solution)/shard_map/analysis/pallas_call | solution.py:347
  (1 shorter events, 0.0 us)
Async XLA Ops:
  0.0 39.2 %copy-start.2 = (f32[2,64,128]{2,1,0:T(8,128)S(1)}, f32[2,64,128]{2,1,0:T(8,128)}, u32[]{:S(2)}) copy-start(f32[2,64,128]{2,1,0:T(8,128)} %constant.20.clone.refs_8_) | copy-start | bytes 196612
  0.0 39.2 %copy-start.4 = (bf16[32,384]{1,0:T(8,128)(2,1)S(1)}, bf16[32,384]{1,0:T(8,128)(2,1)}, u32[]{:S(2)}) copy-start(bf16[32,384]{1,0:T(8,128)(2,1)} %constant.19.clone.refs_7_) | copy-start | bytes 73732
  0.0 39.2 %copy-start = (bf16[384,256]{1,0:T(8,128)(2,1)S(1)}, bf16[384,256]{1,0:T(8,128)(2,1)}, u32[]{:S(2)}) copy-start(bf16[384,256]{1,0:T(8,128)(2,1)} %constant.18.clone.refs_6_) | copy-start | bytes 589828
  0.0 39.2 %copy-start.1 = (bf16[768,128]{1,0:T(8,128)(2,1)S(1)}, bf16[768,128]{1,0:T(8,128)(2,1)}, u32[]{:S(2)}) copy-start(bf16[768,128]{1,0:T(8,128)(2,1)} %constant.17.clone.refs_5_) | copy-start | bytes 589828
  0.0 39.2 %copy-start.3 = (bf16[128,96]{1,0:T(8,128)(2,1)S(1)}, bf16[128,96]{1,0:T(8,128)(2,1)}, u32[]{:S(2)}) copy-start(bf16[128,96]{1,0:T(8,128)(2,1)} %constant.16.clone.refs_4_) | copy-start | bytes 73732
  0.0 39.2 %copy-start.6 = (f32[5]{0:T(128)S(1)}, f32[5]{0:T(128)}, u32[]{:S(2)}) copy-start(f32[5]{0:T(128)} %param.12) | copy-start | bytes 64
  0.0 39.2 %copy-start.5 = (s32[2048]{0:T(1024)S(1)}, s32[2048]{0:T(1024)}, u32[]{:S(2)}) copy-start(s32[2048]{0:T(1024)} %param.11) | copy-start | bytes 24580

commit v5 on v4

--- a/solution.py
+++ b/solution.py
@@ -181,7 +181,7 @@
 GROUP = 16
 PAIR = 4
 STEP = 32
-AHEAD = 3
+AHEAD = 5
 
 
 def synthesis_kernel(alm_ref, leg_ref, out_ref, keep_ref, alm_buf, acc_ref, row_ref, alm_sem, leg_sem, *, bands):
@@ -312,9 +312,9 @@
         chosen = jnp.where(diagonal, tiled, 0.0).astype(bf16)
         left_ref[slot] = chosen.reshape(pair, 2 * CHUNK, width)
 
-    def out_copy(step, slot):
-        rows = pl.ds(step * pair * CHUNK, pair * CHUNK)
-        return pltpu.make_async_copy(buf_ref.at[slot], out_ref.at[:, rows], sem.at[slot])
+    def out_copy(step, slot, item):
+        rows = pl.ds((step * pair + item) * CHUNK, CHUNK)
+        return pltpu.make_async_copy(buf_ref.at[slot, item], out_ref.at[:, rows], sem.at[slot, item])
 
     build(0, 0)
 
@@ -323,20 +323,22 @@
 
         @pl.when(step >= 2)
         def _():
-            out_copy(step - 2, slot).wait()
-
+            for item in range(pair):
+                out_copy(step - 2, slot, item).wait()
+
+        build(jnp.minimum(step + 1, steps - 1), 1 - slot)
         for item in range(pair):
             rows = pl.ds((step * pair + item) * CHUNK, CHUNK)
             right = keep_ref[rows].reshape(width, l_dev)
             result = mm_pieces(left_ref[slot, item], right) * scale
-            buf_ref[slot, :, item * CHUNK : (item + 1) * CHUNK, :] = result.reshape(2, CHUNK, l_dev).astype(bf16)
-        build(jnp.minimum(step + 1, steps - 1), 1 - slot)
-        out_copy(step, slot).start()
+            buf_ref[slot, item] = result.reshape(2, CHUNK, l_dev).astype(bf16)
+            out_copy(step, slot, item).start()
         return carry
 
     lax.fori_loop(0, steps, one_step, 0)
     for step in range(max(steps - 2, 0), steps):
-        out_copy(step, step % 2).wait()
+        for item in range(pair):
+            out_copy(step, step % 2, item).wait()
 
 
 def analysis(weighted, keep, scale):
@@ -353,8 +355,8 @@
             pltpu.VMEM((2, cycle_count, m_dev), f32),
             pltpu.VMEM((chunks, 2, CHUNK, cycle_count), bf16),
             pltpu.VMEM((2, pair, 2 * CHUNK, CHUNK * cycle_count), bf16),
-            pltpu.VMEM((2, 2, pair * CHUNK, l_dev), bf16),
-            pltpu.SemaphoreType.DMA((2,)),
+            pltpu.VMEM((2, pair, 2, CHUNK, l_dev), bf16),
+            pltpu.SemaphoreType.DMA((2, pair)),
         ],
         compiler_params=pltpu.CompilerParams(vmem_limit_bytes=14 * 2**20),
         name="analysis",

time: 62.3 us -> 62.4 us (level)
  no operation moved by 1% of the time
where the time goes in v5:
time: 62.4 us; the launch traced here: 62.2 us
  blocking collectives  32.7 us (52%)
  Pallas kernels  29.3 us (47%)
    pallas_call x1, Pallas kernels, synthesis(): pl.pallas_call(lambda *refs: synthesis_kernel(*refs, bands=bands), out_sh...  17.3 us
    all_to_all x1, blocking collectives, shards(): incoming = lax.all_to_all(outgoing, 'blk', 0, 0, tiled=True)  16 us
    all_to_all x1, blocking collectives, shards(): weighted = lax.all_to_all(copies, 'blk', 0, 0, tiled=True)  10.9 us
    pallas_call x1, Pallas kernels, analysis(): pl.pallas_call(lambda *refs: analysis_kernel(*refs, scale=scale), out_sha...  7.96 us
    all_gather x1, blocking collectives, shards(): gathered = lax.all_gather(spectra, 'mblk', axis=0)  5.78 us
    pallas_call x1, Pallas kernels, band_step(): pl.pallas_call(lambda *refs: band_kernel(*refs, order_count=order_count,...  4.12 us

profile of v5, /device:TPU:0, one launch (start us, length us, event | category | flops | bytes accessed | tf_op | source)
XLA Modules:
  0.0 62.2 jit_solution(8873282672999903188)
XLA Ops:
  0.0 0.0 copy-start.2
  0.0 0.0 copy-start.4
  0.0 0.0 copy-start
  0.0 0.0 copy-start.1
  0.0 0.0 copy-start.3
  0.0 0.0 copy-start.6
  0.0 0.0 copy-start.5
  0.0 17.3 %synthesis.1 = (bf16[8,30,512]{2,1,0:T(8,128)(2,1)S(1)}, bf16[512,40,1024]{2,1,0:T(8,128)(2,1)S(1)}) custom-call(bf16[6,512,1024]{2,1,0:T(8,128)(2,1)} %bitcast.7, bf16[512,40,1024]{2,1,0:T(8,128)(2,1)} %refs_1_.1), custom_call_target="tpu_custom_call" | custom-call | tf_op jit(solution)/shard_map/synthesis/pallas_call | solution.py:266
  17.3 16.0 %all_to_all.10 = bf16[8,30,512]{2,1,0:T(8,128)(2,1)S(1)} all-to-all(bf16[8,30,512]{2,1,0:T(8,128)(2,1)S(1)} %get-tuple-element.12), channel_id=1, replica_groups=mesh['blk'=8,'mblk'=4] {'blk'}, dimensions={0} | all-to-all | bytes 491520 | tf_op jit(solution)/shard_map/all_to_all | solution.py:375
  33.4 5.8 %all-gather.1.refs_1_ = f32[4,30,512]{2,1,0:T(8,128)S(1)} all-gather(f32[1,30,512]{2,1,0:T(8,128)S(1)} %bitcast.8), channel_id=2, replica_groups=mesh['blk'=8,'mblk'=4] {'mblk'}, dimensions={0}, use_global_device_ids=true | all-gather | bytes 307200 | tf_op jit(solution)/shard_map/all_gather | solution.py:377
  39.2 0.0 copy-done.2
  39.2 0.0 copy-done.4
  39.2 0.0 copy-done
  39.2 0.0 copy-done.1
  39.2 0.0 copy-done.3
  39.2 0.0 copy-done.6
  39.2 0.0 copy-done.5
  39.2 4.1 %band.1 = bf16[8,10,512]{2,1,0:T(8,128)(2,1)S(1)} custom-call(s32[1]{0:T(128)} %bitcast.1.refs_0_, f32[4,30,512]{2,1,0:T(8,128)S(1)} %all-gather.1.refs_1_, s32[1,2048]{1,0:T(1,128)S(1)} %bitcast.5, f32[1,5]{1,0:T(1,128)S(1)} %bitcast.6, bf16[128,96]{1,0:T(8,128)(2,1)S(1)} %copy-done.3, bf16[768,128]{1,0:T(8,128)(2,1)S(1)} %copy-done.1, ...), custom_call_target="tpu_custom_call" | custom-call | tf_op jit(solution)/shard_map/band/pallas_call | solution.py:169
  43.3 10.9 %all_to_all.11.refs_0_ = bf16[8,10,512]{2,1,0:T(8,128)(2,1)S(1)} all-to-all(bf16[8,10,512]{2,1,0:T(8,128)(2,1)S(1)} %band.1), channel_id=1, replica_groups=mesh['blk'=8,'mblk'=4] {'blk'}, dimensions={0} | all-to-all | bytes 163840 | tf_op jit(solution)/shard_map/all_to_all | solution.py:379
  54.2 8.0 %analysis.1 = bf16[2,512,1024]{2,1,0:T(8,128)(2,1)} custom-call(bf16[8,10,512]{2,1,0:T(8,128)(2,1)S(1)} %all_to_all.11.refs_0_, bf16[512,40,1024]{2,1,0:T(8,128)(2,1)S(1)} %get-tuple-element.14.refs_1_), custom_call_target="tpu_custom_call" | custom-call | tf_op jit(solution)/shard_map/analysis/pallas_call | solution.py:349
  (1 shorter events, 0.0 us)
Async XLA Ops:
  0.0 39.2 %copy-start.2 = (f32[2,64,128]{2,1,0:T(8,128)S(1)}, f32[2,64,128]{2,1,0:T(8,128)}, u32[]{:S(2)}) copy-start(f32[2,64,128]{2,1,0:T(8,128)} %constant.20.clone.refs_8_) | copy-start | bytes 196612
  0.0 39.2 %copy-start.4 = (bf16[32,384]{1,0:T(8,128)(2,1)S(1)}, bf16[32,384]{1,0:T(8,128)(2,1)}, u32[]{:S(2)}) copy-start(bf16[32,384]{1,0:T(8,128)(2,1)} %constant.19.clone.refs_7_) | copy-start | bytes 73732
  0.0 39.2 %copy-start = (bf16[384,256]{1,0:T(8,128)(2,1)S(1)}, bf16[384,256]{1,0:T(8,128)(2,1)}, u32[]{:S(2)}) copy-start(bf16[384,256]{1,0:T(8,128)(2,1)} %constant.18.clone.refs_6_) | copy-start | bytes 589828
  0.0 39.2 %copy-start.1 = (bf16[768,128]{1,0:T(8,128)(2,1)S(1)}, bf16[768,128]{1,0:T(8,128)(2,1)}, u32[]{:S(2)}) copy-start(bf16[768,128]{1,0:T(8,128)(2,1)} %constant.17.clone.refs_5_) | copy-start | bytes 589828
  0.0 39.2 %copy-start.3 = (bf16[128,96]{1,0:T(8,128)(2,1)S(1)}, bf16[128,96]{1,0:T(8,128)(2,1)}, u32[]{:S(2)}) copy-start(bf16[128,96]{1,0:T(8,128)(2,1)} %constant.16.clone.refs_4_) | copy-start | bytes 73732
  0.0 39.2 %copy-start.6 = (f32[5]{0:T(128)S(1)}, f32[5]{0:T(128)}, u32[]{:S(2)}) copy-start(f32[5]{0:T(128)} %param.12) | copy-start | bytes 64
  0.0 39.2 %copy-start.5 = (s32[2048]{0:T(1024)S(1)}, s32[2048]{0:T(1024)}, u32[]{:S(2)}) copy-start(s32[2048]{0:T(1024)} %param.11) | copy-start | bytes 24580
